TPU v7x, 32 devices: a whole 2x2x4 slice. The times are simulated.
32 devices in a mesh: gx: 2 (over x), gy: 4 (over y, core), gz: 4 (over z).
Axes of the slice: x: 2, y: 2, z: 4, core: 2. Of those that a mesh axis runs over, the one named last changes fastest.
Arguments:
- solid_state: float32 [9, 32, 16, 512], P(None, 'gz', 'gx', 'gy'), may hold values from -6 to 6
- material: float32 [4, 32, 16, 512], P(None, 'gz', 'gx', 'gy'), may hold values from 0.5 to 2
- ocean_state: float32 [4, 16, 32, 1024], P(None, None, 'gx', ('gy', 'gz')), may hold values from -6 to 6
- ocean_medium: float32 [2, 16], replicated, may hold values from 0.5 to 2
- offset_x: int32 [32], P('gx'), may hold values from -1 to 1
- offset_y: int32 [1024], P(('gy', 'gz')), may hold values from -1 to 1
Outputs:
- solid_next: float32 [9, 32, 16, 512], P(None, 'gz', 'gx', 'gy')
- solid_rate: float32 [9, 32, 16, 512], P(None, 'gz', 'gx', 'gy')
- ocean_next: float32 [4, 16, 32, 1024], P(None, None, 'gx', ('gy', 'gz'))
- ocean_rate: float32 [4, 16, 32, 1024], P(None, None, 'gx', ('gy', 'gz'))
All inputs are finite; a program needn't handle non-finite values.
Results may differ from a plain program's by a relative error of at most 0.000059.
Values sent between devices are 32-bit elements; how exact they have to be, the bound alone decides.
No kernel may reach another device: no remote copies, remote signals or barrier semaphores. Data moves between devices by JAX's collectives and lax.ppermute only.
A program may use at most 64 MiB of HBM per device.

v0:
```python
import jax
import jax.numpy as jnp
from jax import lax
from jax.sharding import PartitionSpec as P

closure_rows = (
    (-24.0 / 17.0, 59.0 / 34.0, -4.0 / 17.0, -3.0 / 34.0, 0.0, 0.0),
    (-0.5, 0.0, 0.5, 0.0, 0.0, 0.0),
    (4.0 / 43.0, -59.0 / 86.0, 0.0, 59.0 / 86.0, -4.0 / 43.0, 0.0),
    (3.0 / 98.0, 0.0, -59.0 / 98.0, 0.0, 32.0 / 49.0, -4.0 / 49.0),
)
inv_norm = 48.0 / 17.0
step_size = 0.25
section_weight = 0.1496590219993
gravity = 0.4


def with_halo(x, sides, width):
    for axis, dim in sides:
        size, length = (lax.axis_size(axis), x.shape[dim])
        up = [(i, (i + 1) % size) for i in range(size - 1)]
        down = [(j, i) for i, j in up]
        last = lax.slice_in_dim(x, length - width, length, axis=dim)
        leading = lax.slice_in_dim(x, 0, width, axis=dim)
        before = lax.ppermute(last, axis, up)
        after = lax.ppermute(leading, axis, down)
        x = jnp.concatenate([before, x, after], axis=dim)
    return x


def broadcast(block, axis, owner):
    block = jnp.where(lax.axis_index(axis) == owner, block, jnp.zeros_like(block))
    return lax.psum(block, axis)


def take_slab(field, first_index, length, dimension):
    return lax.slice_in_dim(field, first_index, first_index + length, axis=dimension)


def closure(field, dimension, at_end):
    extent = field.shape[dimension]
    pieces = []
    for row_index in range(4):
        running = jnp.zeros_like(take_slab(field, 0, 1, dimension))
        for col_index in range(6):
            weight = closure_rows[row_index][col_index]
            if weight != 0.0:
                if at_end:
                    running = running - weight * take_slab(
                        field, extent - 1 - col_index, 1, dimension
                    )
                else:
                    running = running + weight * take_slab(field, col_index, 1, dimension)
        pieces.append(running)
    if at_end:
        pieces = pieces[::-1]
    return jnp.concatenate(pieces, axis=dimension)


def interior(padded, dimension, extent):
    return (
        take_slab(padded, 0, extent, dimension)
        - 8.0 * take_slab(padded, 1, extent, dimension)
        + 8.0 * take_slab(padded, 3, extent, dimension)
        - take_slab(padded, 4, extent, dimension)
    ) / 12.0


def derivative(field, dimension):
    extent = field.shape[dimension]
    widths = [(0, 0)] * field.ndim
    widths[dimension] = (2, 2)
    middle = interior(jnp.pad(field, widths), dimension, extent)
    return jnp.concatenate(
        [
            closure(field, dimension, False),
            take_slab(middle, 4, extent - 8, dimension),
            closure(field, dimension, True),
        ],
        axis=dimension,
    )


def local_derivative(padded, field, dimension, is_first, is_last):
    extent = field.shape[dimension]
    middle = interior(padded, dimension, extent)
    head = jnp.where(is_first, closure(field, dimension, False), take_slab(middle, 0, 4, dimension))
    tail = jnp.where(
        is_last, closure(field, dimension, True), take_slab(middle, extent - 4, 4, dimension)
    )
    return jnp.concatenate(
        [head, take_slab(middle, 4, extent - 8, dimension), tail], axis=dimension
    )


def blend_matrix(offsets, fine_first, coarse_first, columns, coarse_total):
    fine_index = fine_first + jnp.arange(offsets.shape[0], dtype=jnp.int32)
    coarse = fine_index // 2
    target = jnp.clip(coarse + offsets, 0, coarse_total - 1)
    column = jnp.arange(columns, dtype=jnp.int32)[None, :]
    nearest = (column == (coarse - coarse_first)[:, None]).astype(jnp.float32)
    farther = (column == (target - coarse_first)[:, None]).astype(jnp.float32)
    return 0.75 * nearest + 0.25 * farther


def restrict(bottom):
    fine_rows, fine_cols = bottom.shape
    return bottom.reshape(fine_rows // 2, 2, fine_cols // 2, 2).mean(axis=(1, 3))


def solid_rates(material, diff_x, diff_y, diff_z):
    buoyancy = material[0]
    lame_one = material[1]
    lame_two = material[2]
    metric = material[3]

    def vertical(member):
        return metric * diff_z(member)

    strain_xx = diff_x(0)
    strain_yy = diff_y(1)
    strain_zz = vertical(2)
    dilation = strain_xx + strain_yy + strain_zz
    return [
        buoyancy * (diff_x(3) + diff_y(8) + vertical(7)),
        buoyancy * (diff_x(8) + diff_y(4) + vertical(6)),
        buoyancy * (diff_x(7) + diff_y(6) + vertical(5)),
        lame_one * dilation + 2.0 * lame_two * strain_xx,
        lame_one * dilation + 2.0 * lame_two * strain_yy,
        lame_one * dilation + 2.0 * lame_two * strain_zz,
        lame_two * (vertical(1) + diff_y(2)),
        lame_two * (vertical(0) + diff_x(2)),
        lame_two * (diff_y(0) + diff_x(1)),
    ]


def seafloor_terms(state, material, bed_pressure):
    factor = inv_norm * material[0, 0] * material[3, 0]
    return (factor * state[7, 0], factor * state[6, 0], factor * (state[5, 0] + bed_pressure))


def ocean_rates(state, medium, diff_x, diff_y, bed_speed):
    bulk = medium[0][:, None, None]
    light = medium[1][:, None, None]
    pressure = state[0]
    flow_z = state[3]
    rate_p = (
        -bulk * (2.0 * diff_x(1) + 2.0 * diff_y(2) + derivative(flow_z, 0))
        + gravity * flow_z / light
    )
    rate_p = rate_p.at[-1].add(inv_norm * bulk[-1] * (flow_z[-1] - bed_speed))
    rate_u = -2.0 * light * diff_x(0)
    rate_v = -2.0 * light * diff_y(0)
    rate_w = -light * derivative(pressure, 0)
    rate_w = rate_w.at[0].add(-inv_norm * light[0] * pressure[0])
    return jnp.stack([rate_p, rate_u, rate_v, rate_w])


def body(solid_state, material, ocean_state, ocean_medium, offset_x, offset_y):
    highest = lax.Precision.HIGHEST
    span_x = lax.axis_size("gx")
    span_y = lax.axis_size("gy")
    span_z = lax.axis_size("gz")
    index_x = lax.axis_index("gx")
    index_y = lax.axis_index("gy")
    index_z = lax.axis_index("gz")
    cells_x = solid_state.shape[2]
    cells_y = solid_state.shape[3]
    column_width = ocean_state.shape[3]
    x_first = index_x == 0
    x_last = index_x == span_x - 1
    y_first = index_y == 0
    y_last = index_y == span_y - 1
    z_first = index_z == 0
    z_last = index_z == span_z - 1
    joint_first = jnp.logical_and(y_first, z_first)
    joint_last = jnp.logical_and(y_last, z_last)
    plane = solid_state[2, 0]
    rimmed = with_halo(plane, (("gx", 0), ("gy", 1)), 1)
    shared = broadcast(rimmed, "gz", 0)
    bottom_part = restrict(ocean_state[0, -1])
    bed_pressure = lax.all_gather(bottom_part, "gz", axis=1, tiled=True)
    ocean_rim = with_halo(ocean_state[0:3], (("gx", 2), (("gy", "gz"), 3)), 2)
    x_fields = (0, 1, 2, 3, 8, 7)
    y_fields = (0, 1, 2, 4, 8, 6)
    z_fields = (0, 1, 2, 5, 6, 7)
    sent_x = with_halo(jnp.stack([solid_state[member] for member in x_fields]), (("gx", 2),), 2)
    sent_y = with_halo(jnp.stack([solid_state[member] for member in y_fields]), (("gy", 3),), 2)
    sent_z = with_halo(jnp.stack([solid_state[member] for member in z_fields]), (("gz", 1),), 2)

    def padded_x(member):
        return sent_x[x_fields.index(member)]

    def padded_y(member):
        return sent_y[y_fields.index(member)]

    def padded_z(member):
        return sent_z[z_fields.index(member)]

    rates = solid_rates(
        material,
        lambda member: local_derivative(padded_x(member), solid_state[member], 1, x_first, x_last),
        lambda member: local_derivative(padded_y(member), solid_state[member], 2, y_first, y_last),
        lambda member: local_derivative(padded_z(member), solid_state[member], 0, z_first, z_last),
    )
    term_x, term_y, term_z = seafloor_terms(solid_state, material, bed_pressure)
    rates[0] = rates[0].at[0].add(jnp.where(z_first, term_x, 0.0))
    rates[1] = rates[1].at[0].add(jnp.where(z_first, term_y, 0.0))
    rates[2] = rates[2].at[0].add(jnp.where(z_first, term_z, 0.0))
    solid_rate = step_size * jnp.stack(rates)
    solid_next = solid_state + section_weight * solid_rate
    blend_x = blend_matrix(
        offset_x, index_x * 2 * cells_x, index_x * cells_x - 1, cells_x + 2, cells_x * span_x
    )
    blend_y = blend_matrix(
        offset_y,
        index_y * 2 * cells_y + index_z * column_width,
        index_y * cells_y - 1,
        cells_y + 2,
        cells_y * span_y,
    )
    bed_speed = jnp.dot(jnp.dot(blend_x, shared, precision=highest), blend_y.T, precision=highest)
    ocean_rate = step_size * ocean_rates(
        ocean_state,
        ocean_medium,
        lambda member: local_derivative(
            ocean_rim[member, :, :, 2:-2], ocean_state[member], 1, x_first, x_last
        ),
        lambda member: local_derivative(
            ocean_rim[member, :, 2:-2, :], ocean_state[member], 2, joint_first, joint_last
        ),
        bed_speed,
    )
    ocean_next = ocean_state + section_weight * ocean_rate
    return (solid_next, solid_rate, ocean_next, ocean_rate)


def solution(mesh):
    in_specs = (
        P(None, "gz", "gx", "gy"),
        P(None, "gz", "gx", "gy"),
        P(None, None, "gx", ("gy", "gz")),
        P(),
        P("gx"),
        P(("gy", "gz")),
    )
    out_specs = (
        P(None, "gz", "gx", "gy"),
        P(None, "gz", "gx", "gy"),
        P(None, None, "gx", ("gy", "gz")),
        P(None, None, "gx", ("gy", "gz")),
    )
    return jax.shard_map(body, mesh=mesh, in_specs=in_specs, out_specs=out_specs, check_vma=False)
```

profile of v0, /device:TPU:14, one launch (start us, length us, event | category | flops | bytes accessed | tf_op | source)
XLA Modules:
  0.0 214.7 jit_solution(6294805913132325502)
XLA Ops:
  0.6 1.7 fusion.201
  2.3 1.3 collective-permute-start.6
  3.6 5.8 %collective-permute-start.7 = (f32[3,16,2,64]{3,2,1,0:T(2,128)}, f32[3,16,2,64]{3,2,1,0:T(2,128)}, u32[]{:S(2)}, u32[]{:S(2)}) collective-permute-start(f32[3,16,2,64]{3,2,1,0:T(2,128)} %get-tuple-element.115), channel_id=1, source_target_pairs={{16,0},{17,1},{18,2},{19,3},{20,4},{21,5},{22,6},{23,7},{24,8},{25... | collective-permute-start | bytes 73736 | tf_op jit(solution)/shard_map/ppermute | solution.py:26
  9.4 1.3 slice_bitcast_fusion.42
  10.7 1.3 collective-permute-start.10
  12.0 5.8 %collective-permute-start.11 = (f32[1,128]{1,0:T(1,128)}, f32[1,128]{1,0:T(1,128)}, u32[]{:S(2)}, u32[]{:S(2)}) collective-permute-start(f32[1,128]{1,0:T(1,128)} %get-tuple-element.135), channel_id=1, source_target_pairs={{16,0},{17,1},{18,2},{19,3},{20,4},{21,5},{22,6},{23,7},{24,8},{25... | collective-permute-start | bytes 1544 | tf_op jit(solution)/shard_map/ppermute | solution.py:26
  17.8 1.5 slice_bitcast_fusion.23
  20.7 1.3 collective-permute-start
  22.0 1.7 slice_multiply_fusion.35
  49.0 1.1 copy.451
  50.2 1.1 copy.454
  51.3 1.1 copy.456
  52.6 1.1 copy.464
  53.7 1.1 copy.466
  70.9 13.4 %all-gather = f32[4,32,8]{1,2,0:T(8,128)S(1)} all-gather(f32[1,32,8]{1,2,0:T(8,128)S(1)} %multiply_bitcast_fusion), channel_id=1, replica_groups=mesh['gx'=2,'gy'=4,'gz'=4] {'gz'}, dimensions={0}, use_global_device_ids=true | all-gather | bytes 5120 | tf_op jit(solution)/shard_map/all_gather | solution.py:182
  97.0 1.9 collective-permute-start.2
  99.7 1.9 collective-permute-start.12
  101.6 3.0 %collective-permute-done.12 = f32[10,1]{1,0:T(8,128)S(1)} collective-permute-done((f32[10,1]{1,0:T(8,128)S(1)}, f32[10,1]{1,0:T(8,128)S(1)}, u32[]{:S(2)}, u32[]{:S(2)}) %collective-permute-start.12) | collective-permute-done | bytes 72 | tf_op jit(solution)/shard_map/ppermute | solution.py:25
  104.7 1.9 collective-permute-start.13
  106.6 1.3 collective-permute-done.13
  107.9 3.6 %collective-permute-start.3 = (f32[6,8,8,2]{3,2,1,0:T(8,128)S(1)}, f32[6,8,8,2]{3,2,1,0:T(8,128)S(1)}, u32[]{:S(2)}, u32[]{:S(2)}) collective-permute-start(f32[6,8,8,2]{3,2,1,0:T(8,128)S(1)} %get-tuple-element.208), channel_id=1, source_target_pairs={{4,0},{8,4},{12,8},{5,1},{9,5},{13,9},{6,2},{10,6},{14,10},{7,3},{... | collective-permute-start | bytes 9224 | tf_op jit(solution)/shard_map/ppermute | solution.py:26
  112.3 15.1 %psum.7 = f32[10,130]{1,0:T(8,128)S(1)} all-reduce(f32[10,130]{1,0:T(8,128)S(1)} %maximum_select_fusion.3), channel_id=1, replica_groups=mesh['gx'=2,'gy'=4,'gz'=4] {'gz'}, use_global_device_ids=true, to_apply=%region_1.2 | all-reduce | flops 1300 | bytes 10400 | tf_op jit(solution)/shard_map/psum | solution.py:33
  128.3 5.8 %collective-permute-start.1 = (f32[6,8,2,128]{3,2,1,0:T(2,128)}, f32[6,8,2,128]{3,2,1,0:T(2,128)}, u32[]{:S(2)}, u32[]{:S(2)}) collective-permute-start(f32[6,8,2,128]{3,2,1,0:T(2,128)} %get-tuple-element.210), channel_id=1, source_target_pairs={{16,0},{17,1},{18,2},{19,3},{20,4},{21,5},{22,6},{23,7},{24,8},{25... | collective-permute-start | bytes 147464 | tf_op jit(solution)/shard_map/ppermute | solution.py:26
  134.0 4.1 %collective-permute-start.4 = (f32[6,2,8,128]{3,2,1,0:T(8,128)}, f32[6,2,8,128]{3,2,1,0:T(8,128)}, u32[]{:S(2)}, u32[]{:S(2)}) collective-permute-start(f32[6,2,8,128]{3,2,1,0:T(8,128)} %get-tuple-element.205), channel_id=1, source_target_pairs={{0,1},{1,2},{2,3},{4,5},{5,6},{6,7},{8,9},{9,10},{10,11},{12,13},{... | collective-permute-start | bytes 147464 | tf_op jit(solution)/shard_map/ppermute | solution.py:25
  150.6 1.0 copy.436
  151.6 2.6 %collective-permute-start.8 = (f32[3,16,20,2]{2,1,3,0:T(8,128)}, f32[3,16,20,2]{2,1,3,0:T(8,128)S(1)}, u32[]{:S(2)}, u32[]{:S(2)}) collective-permute-start(f32[3,16,20,2]{2,1,3,0:T(8,128)} %copy.436), channel_id=1, source_target_pairs={{0,1},{1,2},{2,3},{3,4},{4,5},{5,6},{6,7},{7,8},{8,9},{9,10},{10,1... | collective-permute-start | bytes 23048 | tf_op jit(solution)/shard_map/ppermute | solution.py:25
  154.6 3.2 %collective-permute-start.9 = (f32[3,16,20,2]{2,1,3,0:T(8,128)S(1)}, f32[3,16,20,2]{2,1,3,0:T(8,128)}, u32[]{:S(2)}, u32[]{:S(2)}) collective-permute-start(f32[3,16,20,2]{2,1,3,0:T(8,128)S(1)} %copy.437), channel_id=1, source_target_pairs={{1,0},{2,1},{3,2},{4,3},{5,4},{6,5},{7,6},{8,7},{9,8},{10,9},{11,1... | collective-permute-start | bytes 23048 | tf_op jit(solution)/shard_map/ppermute | solution.py:26
  160.2 6.3 %collective-permute-start.5 = (f32[6,2,8,128]{3,2,1,0:T(8,128)}, f32[6,2,8,128]{3,2,1,0:T(8,128)}, u32[]{:S(2)}, u32[]{:S(2)}) collective-permute-start(f32[6,2,8,128]{3,2,1,0:T(8,128)} %get-tuple-element.206), channel_id=1, source_target_pairs={{1,0},{2,1},{3,2},{5,4},{6,5},{7,6},{9,8},{10,9},{11,10},{13,12},{... | collective-permute-start | bytes 147464 | tf_op jit(solution)/shard_map/ppermute | solution.py:26
  166.9 1.2 copy.439
  171.3 1.5 slice_multiply_fusion.23
  172.8 1.1 slice_multiply_fusion.51
  175.4 2.2 %fusion.4 = f32[1,16,16,64]{3,2,1,0:T(8,128)S(1)} fusion(f32[1,16,16,64]{3,2,1,0:T(8,128)S(1)} %get-tuple-element.104, f32[16,130]{1,0:T(8,128)S(1)} %copy-done.253, s32[64]{0:T(128)S(1)} %copy-done.264, s32[64]{0:T(128)S(1)} %copy-done.265, f32[16,16,64]{2,1,0:T(8,128)S(1)} %get-tuple-element.107, f32[16,16,64]{2,1,0:T(8,128)} %copy-done.258, ...), kind=kOutput, calls=%fused_computation.5 | convolution fusion | flops 1653376 | bytes 570380 | tf_op jit(solution)/shard_map/dot_general | solution.py:222
  (843 shorter events, 111.1 us)
Async XLA Ops:
  2.3 147.1 %collective-permute-start.6 = (f32[3,16,2,64]{3,2,1,0:T(2,128)}, f32[3,16,2,64]{3,2,1,0:T(2,128)}, u32[]{:S(2)}, u32[]{:S(2)}) collective-permute-start(f32[3,16,2,64]{3,2,1,0:T(2,128)} %get-tuple-element.114), channel_id=1, source_target_pairs={{0,16},{1,17},{2,18},{3,19},{4,20},{5,21},{6,22},{7,23},{8,24},{9,... | collective-permute-start | bytes 73736 | tf_op jit(solution)/shard_map/ppermute | solution.py:25
  3.6 145.8 %collective-permute-start.7 = (f32[3,16,2,64]{3,2,1,0:T(2,128)}, f32[3,16,2,64]{3,2,1,0:T(2,128)}, u32[]{:S(2)}, u32[]{:S(2)}) collective-permute-start(f32[3,16,2,64]{3,2,1,0:T(2,128)} %get-tuple-element.115), channel_id=1, source_target_pairs={{16,0},{17,1},{18,2},{19,3},{20,4},{21,5},{22,6},{23,7},{24,8},{25... | collective-permute-start | bytes 73736 | tf_op jit(solution)/shard_map/ppermute | solution.py:26
  10.7 86.3 %collective-permute-start.10 = (f32[1,128]{1,0:T(1,128)}, f32[1,128]{1,0:T(1,128)}, u32[]{:S(2)}, u32[]{:S(2)}) collective-permute-start(f32[1,128]{1,0:T(1,128)} %get-tuple-element.134), channel_id=1, source_target_pairs={{0,16},{1,17},{2,18},{3,19},{4,20},{5,21},{6,22},{7,23},{8,24},{9,... | collective-permute-start | bytes 1544 | tf_op jit(solution)/shard_map/ppermute | solution.py:25
  11.9 7.4 %copy-start.1 = (f32[9,8,8,128]{3,2,1,0:T(8,128)S(1)}, f32[9,8,8,128]{3,2,1,0:T(8,128)}, u32[]{:S(2)}) copy-start(f32[9,8,8,128]{3,2,1,0:T(8,128)} %param.16) | copy-start | bytes 884740
  12.0 87.0 %collective-permute-start.11 = (f32[1,128]{1,0:T(1,128)}, f32[1,128]{1,0:T(1,128)}, u32[]{:S(2)}, u32[]{:S(2)}) collective-permute-start(f32[1,128]{1,0:T(1,128)} %get-tuple-element.135), channel_id=1, source_target_pairs={{16,0},{17,1},{18,2},{19,3},{20,4},{21,5},{22,6},{23,7},{24,8},{25... | collective-permute-start | bytes 1544 | tf_op jit(solution)/shard_map/ppermute | solution.py:26
  20.7 175.5 %collective-permute-start = (f32[6,8,2,128]{3,2,1,0:T(2,128)}, f32[6,8,2,128]{3,2,1,0:T(2,128)}, u32[]{:S(2)}, u32[]{:S(2)}) collective-permute-start(f32[6,8,2,128]{3,2,1,0:T(2,128)} %get-tuple-element.209), channel_id=1, source_target_pairs={{0,16},{1,17},{2,18},{3,19},{4,20},{5,21},{6,22},{7,23},{8,24},{9,... | collective-permute-start | bytes 147464 | tf_op jit(solution)/shard_map/ppermute | solution.py:25
  25.4 40.4 %copy-start.259 = (f32[16]{0:T(128)}, f32[16]{0:T(128)S(1)}, u32[]{:S(2)}) copy-start(f32[16]{0:T(128)S(1)} %get-tuple-element.498) | copy-start | bytes 196
  25.4 41.1 %copy-start.261 = (f32[16]{0:T(128)}, f32[16]{0:T(128)S(1)}, u32[]{:S(2)}) copy-start(f32[16]{0:T(128)S(1)} %get-tuple-element.499) | copy-start | bytes 196
  70.9 14.1 %copy-start.94 = (f32[8,8,1]{2,1,0:T(8,128)S(1)}, f32[8,8,1]{2,1,0:T(8,128)}, u32[]{:S(2)}) copy-start(f32[8,8,1]{2,1,0:T(8,128)} %get-tuple-element.420) | copy-start | bytes 772
  88.1 6.2 %copy-start.243 = (f32[8,1,128]{2,1,0:T(1,128)S(1)}, f32[8,1,128]{2,1,0:T(1,128)}, u32[]{:S(2)}) copy-start(f32[8,1,128]{2,1,0:T(1,128)} %get-tuple-element.360) | copy-start | bytes 12292
  88.1 6.2 %copy-start.244 = (f32[8,1,128]{2,1,0:T(1,128)S(1)}, f32[8,1,128]{2,1,0:T(1,128)}, u32[]{:S(2)}) copy-start(f32[8,1,128]{2,1,0:T(1,128)} %get-tuple-element.361) | copy-start | bytes 12292
  88.1 6.2 %copy-start.245 = (f32[8,1,128]{2,1,0:T(1,128)S(1)}, f32[8,1,128]{2,1,0:T(1,128)}, u32[]{:S(2)}) copy-start(f32[8,1,128]{2,1,0:T(1,128)} %get-tuple-element.364) | copy-start | bytes 12292
  88.1 6.2 %copy-start.246 = (f32[8,1,128]{2,1,0:T(1,128)S(1)}, f32[8,1,128]{2,1,0:T(1,128)}, u32[]{:S(2)}) copy-start(f32[8,1,128]{2,1,0:T(1,128)} %get-tuple-element.365) | copy-start | bytes 12292
  88.1 6.2 %copy-start.247 = (f32[8,1,128]{2,1,0:T(1,128)S(1)}, f32[8,1,128]{2,1,0:T(1,128)}, u32[]{:S(2)}) copy-start(f32[8,1,128]{2,1,0:T(1,128)} %get-tuple-element.367) | copy-start | bytes 12292
  88.1 6.2 %copy-start.248 = (f32[8,1,128]{2,1,0:T(1,128)S(1)}, f32[8,1,128]{2,1,0:T(1,128)}, u32[]{:S(2)}) copy-start(f32[8,1,128]{2,1,0:T(1,128)} %get-tuple-element.368) | copy-start | bytes 12292
  88.1 6.2 %copy-start.249 = (f32[8,1,128]{2,1,0:T(1,128)S(1)}, f32[8,1,128]{2,1,0:T(1,128)}, u32[]{:S(2)}) copy-start(f32[8,1,128]{2,1,0:T(1,128)} %get-tuple-element.369) | copy-start | bytes 12292
  88.2 5.4 %copy-start.226 = (f32[8,1,128]{2,1,0:T(1,128)S(1)}, f32[8,1,128]{2,1,0:T(1,128)}, u32[]{:S(2)}) copy-start(f32[8,1,128]{2,1,0:T(1,128)} %get-tuple-element.340) | copy-start | bytes 12292
  88.2 5.4 %copy-start.227 = (f32[8,1,128]{2,1,0:T(1,128)S(1)}, f32[8,1,128]{2,1,0:T(1,128)}, u32[]{:S(2)}) copy-start(f32[8,1,128]{2,1,0:T(1,128)} %get-tuple-element.399) | copy-start | bytes 12292
  89.0 5.9 %copy-start.74 = (f32[8,8,1]{2,1,0:T(8,128)S(1)}, f32[8,8,1]{2,1,0:T(8,128)}, u32[]{:S(2)}) copy-start(f32[8,8,1]{2,1,0:T(8,128)} %get-tuple-element.391) | copy-start | bytes 772
  97.0 31.3 %collective-permute-start.2 = (f32[6,8,8,2]{3,2,1,0:T(8,128)S(1)}, f32[6,8,8,2]{3,2,1,0:T(8,128)S(1)}, u32[]{:S(2)}, u32[]{:S(2)}) collective-permute-start(f32[6,8,8,2]{3,2,1,0:T(8,128)S(1)} %get-tuple-element.207), channel_id=1, source_target_pairs={{0,4},{4,8},{8,12},{1,5},{5,9},{9,13},{2,6},{6,10},{10,14},{3,7},{... | collective-permute-start | bytes 9224 | tf_op jit(solution)/shard_map/ppermute | solution.py:25
  99.7 5.0 %collective-permute-start.12 = (f32[10,1]{1,0:T(8,128)S(1)}, f32[10,1]{1,0:T(8,128)S(1)}, u32[]{:S(2)}, u32[]{:S(2)}) collective-permute-start(f32[10,1]{1,0:T(8,128)S(1)} %get-tuple-element.492), channel_id=1, source_target_pairs={{0,4},{4,8},{8,12},{1,5},{5,9},{9,13},{2,6},{6,10},{10,14},{3,7},{... | collective-permute-start | bytes 128 | tf_op jit(solution)/shard_map/ppermute | solution.py:25
  104.7 3.3 %collective-permute-start.13 = (f32[10,1]{1,0:T(8,128)S(1)}, f32[10,1]{1,0:T(8,128)S(1)}, u32[]{:S(2)}, u32[]{:S(2)}) collective-permute-start(f32[10,1]{1,0:T(8,128)S(1)} %get-tuple-element.493), channel_id=1, source_target_pairs={{4,0},{8,4},{12,8},{5,1},{9,5},{13,9},{6,2},{10,6},{14,10},{7,3},{... | collective-permute-start | bytes 128 | tf_op jit(solution)/shard_map/ppermute | solution.py:26
  107.9 26.1 %collective-permute-start.3 = (f32[6,8,8,2]{3,2,1,0:T(8,128)S(1)}, f32[6,8,8,2]{3,2,1,0:T(8,128)S(1)}, u32[]{:S(2)}, u32[]{:S(2)}) collective-permute-start(f32[6,8,8,2]{3,2,1,0:T(8,128)S(1)} %get-tuple-element.208), channel_id=1, source_target_pairs={{4,0},{8,4},{12,8},{5,1},{9,5},{13,9},{6,2},{10,6},{14,10},{7,3},{... | collective-permute-start | bytes 9224 | tf_op jit(solution)/shard_map/ppermute | solution.py:26
  127.4 10.7 %copy-start.34 = (f32[1,8,8,128]{3,2,1,0:T(8,128)S(1)}, f32[1,8,8,128]{3,2,1,0:T(8,128)}, u32[]{:S(2)}) copy-start(f32[1,8,8,128]{3,2,1,0:T(8,128)} %copy-done.33) | copy-start | bytes 98308
  127.4 10.7 %copy-start.36 = (f32[1,8,8,128]{3,2,1,0:T(8,128)S(1)}, f32[1,8,8,128]{3,2,1,0:T(8,128)}, u32[]{:S(2)}) copy-start(f32[1,8,8,128]{3,2,1,0:T(8,128)} %copy-done.35) | copy-start | bytes 98308
  128.3 67.9 %collective-permute-start.1 = (f32[6,8,2,128]{3,2,1,0:T(2,128)}, f32[6,8,2,128]{3,2,1,0:T(2,128)}, u32[]{:S(2)}, u32[]{:S(2)}) collective-permute-start(f32[6,8,2,128]{3,2,1,0:T(2,128)} %get-tuple-element.210), channel_id=1, source_target_pairs={{16,0},{17,1},{18,2},{19,3},{20,4},{21,5},{22,6},{23,7},{24,8},{25... | collective-permute-start | bytes 147464 | tf_op jit(solution)/shard_map/ppermute | solution.py:26
  134.0 61.2 %collective-permute-start.4 = (f32[6,2,8,128]{3,2,1,0:T(8,128)}, f32[6,2,8,128]{3,2,1,0:T(8,128)}, u32[]{:S(2)}, u32[]{:S(2)}) collective-permute-start(f32[6,2,8,128]{3,2,1,0:T(8,128)} %get-tuple-element.205), channel_id=1, source_target_pairs={{0,1},{1,2},{2,3},{4,5},{5,6},{6,7},{8,9},{9,10},{10,11},{12,13},{... | collective-permute-start | bytes 147464 | tf_op jit(solution)/shard_map/ppermute | solution.py:25
  151.6 8.5 %collective-permute-start.8 = (f32[3,16,20,2]{2,1,3,0:T(8,128)}, f32[3,16,20,2]{2,1,3,0:T(8,128)S(1)}, u32[]{:S(2)}, u32[]{:S(2)}) collective-permute-start(f32[3,16,20,2]{2,1,3,0:T(8,128)} %copy.436), channel_id=1, source_target_pairs={{0,1},{1,2},{2,3},{3,4},{4,5},{5,6},{6,7},{7,8},{8,9},{9,10},{10,1... | collective-permute-start | bytes 23048 | tf_op jit(solution)/shard_map/ppermute | solution.py:25
  154.6 12.3 %collective-permute-start.9 = (f32[3,16,20,2]{2,1,3,0:T(8,128)S(1)}, f32[3,16,20,2]{2,1,3,0:T(8,128)}, u32[]{:S(2)}, u32[]{:S(2)}) collective-permute-start(f32[3,16,20,2]{2,1,3,0:T(8,128)S(1)} %copy.437), channel_id=1, source_target_pairs={{1,0},{2,1},{3,2},{4,3},{5,4},{6,5},{7,6},{8,7},{9,8},{10,9},{11,1... | collective-permute-start | bytes 23048 | tf_op jit(solution)/shard_map/ppermute | solution.py:26
  160.1 9.5 %copy-start.52 = (f32[16,4,64]{2,1,0:T(4,128)}, f32[16,4,64]{2,1,0:T(4,128)S(1)}, u32[]{:S(2)}) copy-start(f32[16,4,64]{2,1,0:T(4,128)S(1)} %get-tuple-element.255) | copy-start | bytes 49156
  160.1 9.5 %copy-start.54 = (f32[16,4,64]{2,1,0:T(4,128)}, f32[16,4,64]{2,1,0:T(4,128)S(1)}, u32[]{:S(2)}) copy-start(f32[16,4,64]{2,1,0:T(4,128)S(1)} %get-tuple-element.256) | copy-start | bytes 49156
  160.2 35.0 %collective-permute-start.5 = (f32[6,2,8,128]{3,2,1,0:T(8,128)}, f32[6,2,8,128]{3,2,1,0:T(8,128)}, u32[]{:S(2)}, u32[]{:S(2)}) collective-permute-start(f32[6,2,8,128]{3,2,1,0:T(8,128)} %get-tuple-element.206), channel_id=1, source_target_pairs={{1,0},{2,1},{3,2},{5,4},{6,5},{7,6},{9,8},{10,9},{11,10},{13,12},{... | collective-permute-start | bytes 147464 | tf_op jit(solution)/shard_map/ppermute | solution.py:26
  (250 other events, 307.7 us)
where the time goes:
time: 218 us; the launch traced here: 215 us
  local copies, waits for them, and re-layouts  75.3 us (35%)
  other arithmetic  51.4 us (24%)
  starting transfers between devices  46.8 us (21%)
  blocking collectives  28.6 us (13%)
  between operations  5.11 us (2%)
  waiting for transfers between devices  4.42 us (2%)
  matrix products  3.04 us (1%)
    unnamed x556, local copies, waits for them, and re-layouts  41.2 us
    ppermute x7, starting transfers between devices, with_halo(): after = lax.ppermute(leading, axis, down)  32.4 us
    add x45, other arithmetic, closure(): running = running + weight * take_slab(field, col_index, 1, dimension)  25 us
    psum x1, blocking collectives, broadcast(): return lax.psum(block, axis)  15.1 us
    ppermute x7, starting transfers between devices, with_halo(): before = lax.ppermute(last, axis, up)  14.4 us
    all_gather x1, blocking collectives, body(): bed_pressure = lax.all_gather(bottom_part, 'gz', axis=1, tiled=True)  13.4 us
    mul x20, local copies, waits for them, and re-layouts, closure(): weight * take_slab(field, extent - 1 - col_index, 1, dimension)  6.82 us
    slice x7, local copies, waits for them, and re-layouts, with_halo(): last = lax.slice_in_dim(x, length - width, length, axis=dim)  5.06 us
  transfers between devices with their start and end apart: 14, of which 2 were waited for; matrix products, arithmetic and copies ran while one was open for 41% of the time, Pallas kernels for 0%

commit v1 on v0

--- a/solution.py
+++ b/solution.py
@@ -30,7 +30,7 @@
 
 def broadcast(block, axis, owner):
     block = jnp.where(lax.axis_index(axis) == owner, block, jnp.zeros_like(block))
-    return lax.psum(block, axis)
+    return jnp.sum(lax.all_gather(block, axis), axis=0)
 
 
 def take_slab(field, first_index, length, dimension):

time: 218 us -> 214 us (0.982)
    psum x1 -> x0, blocking collectives: 15.1 us -> none  [broadcast(): return lax.psum(block, axis)]
    all_gather x0 -> x1, blocking collectives: none -> 13.1 us  [broadcast(): return jnp.sum(lax.all_gather(block, axis), axis=0)]
  transfers between devices with their start and end apart: 14 -> 14, of which waited for: 2 -> 2; matrix products, arithmetic and copies ran while one was open for 41% -> 42% of each run, Pallas kernels for 0% -> 0%
where the time goes in v1:
time: 214 us; the launch traced here: 210 us
  local copies, waits for them, and re-layouts  75.2 us (35%)
  other arithmetic  50.7 us (24%)
  starting transfers between devices  45.3 us (21%)
  blocking collectives  26.6 us (12%)
  between operations  5.18 us (2%)
  waiting for transfers between devices  4.42 us (2%)
  matrix products  3.04 us (1%)
    unnamed x556, local copies, waits for them, and re-layouts  41 us
    ppermute x7, starting transfers between devices, with_halo(): after = lax.ppermute(leading, axis, down)  30.9 us
    add x45, other arithmetic, closure(): running = running + weight * take_slab(field, col_index, 1, dimension)  24.9 us
    ppermute x7, starting transfers between devices, with_halo(): before = lax.ppermute(last, axis, up)  14.4 us
    all_gather x1, blocking collectives, body(): bed_pressure = lax.all_gather(bottom_part, 'gz', axis=1, tiled=True)  13.4 us
    all_gather x1, blocking collectives, broadcast(): return jnp.sum(lax.all_gather(block, axis), axis=0)  13.1 us
    mul x20, local copies, waits for them, and re-layouts, closure(): weight * take_slab(field, extent - 1 - col_index, 1, dimension)  6.82 us
    slice x7, local copies, waits for them, and re-layouts, with_halo(): last = lax.slice_in_dim(x, length - width, length, axis=dim)  5.07 us
  transfers between devices with their start and end apart: 14, of which 2 were waited for; matrix products, arithmetic and copies ran while one was open for 42% of the time, Pallas kernels for 0%

profile of v1, /device:TPU:14, one launch (start us, length us, event | category | flops | bytes accessed | tf_op | source)
XLA Modules:
  0.0 210.4 jit_solution(5923803238440442416)
XLA Ops:
  0.6 1.7 fusion.202
  2.3 1.3 collective-permute-start.6
  3.6 5.8 %collective-permute-start.7 = (f32[3,16,2,64]{3,2,1,0:T(2,128)}, f32[3,16,2,64]{3,2,1,0:T(2,128)}, u32[]{:S(2)}, u32[]{:S(2)}) collective-permute-start(f32[3,16,2,64]{3,2,1,0:T(2,128)} %get-tuple-element.115), channel_id=1, source_target_pairs={{16,0},{17,1},{18,2},{19,3},{20,4},{21,5},{22,6},{23,7},{24,8},{25... | collective-permute-start | bytes 73736 | tf_op jit(solution)/shard_map/ppermute | solution.py:26
  9.4 1.3 slice_bitcast_fusion.42
  10.7 1.3 collective-permute-start.10
  12.0 5.7 %collective-permute-start.11 = (f32[1,128]{1,0:T(1,128)}, f32[1,128]{1,0:T(1,128)}, u32[]{:S(2)}, u32[]{:S(2)}) collective-permute-start(f32[1,128]{1,0:T(1,128)} %get-tuple-element.135), channel_id=1, source_target_pairs={{16,0},{17,1},{18,2},{19,3},{20,4},{21,5},{22,6},{23,7},{24,8},{25... | collective-permute-start | bytes 1544 | tf_op jit(solution)/shard_map/ppermute | solution.py:26
  17.7 1.6 slice_bitcast_fusion.23
  20.6 1.3 collective-permute-start
  21.9 1.7 slice_multiply_fusion.35
  48.8 1.1 copy.459
  50.1 1.1 copy.462
  51.2 1.1 copy.464
  52.4 1.1 copy.472
  53.5 1.1 copy.474
  70.8 13.4 %all-gather = f32[4,32,8]{1,2,0:T(8,128)S(1)} all-gather(f32[1,32,8]{1,2,0:T(8,128)S(1)} %multiply_bitcast_fusion), channel_id=1, replica_groups=mesh['gx'=2,'gy'=4,'gz'=4] {'gz'}, dimensions={0}, use_global_device_ids=true | all-gather | bytes 5120 | tf_op jit(solution)/shard_map/all_gather | solution.py:182
  97.0 1.9 collective-permute-start.2
  99.7 1.9 collective-permute-start.12
  101.6 3.0 %collective-permute-done.12 = f32[10,1]{1,0:T(8,128)S(1)} collective-permute-done((f32[10,1]{1,0:T(8,128)S(1)}, f32[10,1]{1,0:T(8,128)S(1)}, u32[]{:S(2)}, u32[]{:S(2)}) %collective-permute-start.12) | collective-permute-done | bytes 72 | tf_op jit(solution)/shard_map/ppermute | solution.py:25
  104.6 1.9 collective-permute-start.13
  106.5 1.3 collective-permute-done.13
  107.9 3.6 %collective-permute-start.3 = (f32[6,8,8,2]{3,2,1,0:T(8,128)S(1)}, f32[6,8,8,2]{3,2,1,0:T(8,128)S(1)}, u32[]{:S(2)}, u32[]{:S(2)}) collective-permute-start(f32[6,8,8,2]{3,2,1,0:T(8,128)S(1)} %get-tuple-element.208), channel_id=1, source_target_pairs={{4,0},{8,4},{12,8},{5,1},{9,5},{13,9},{6,2},{10,6},{14,10},{7,3},{... | collective-permute-start | bytes 9224 | tf_op jit(solution)/shard_map/ppermute | solution.py:26
  111.6 13.1 %all_gather.8 = f32[4,10,130]{2,1,0:T(8,128)S(1)} all-gather(f32[1,10,130]{2,1,0:T(8,128)S(1)} %maximum_select_fusion.3), channel_id=1, replica_groups=mesh['gx'=2,'gy'=4,'gz'=4] {'gz'}, dimensions={0}, use_global_device_ids=true | all-gather | bytes 26000 | tf_op jit(solution)/shard_map/all_gather | solution.py:33
  125.5 5.8 %collective-permute-start.1 = (f32[6,8,2,128]{3,2,1,0:T(2,128)}, f32[6,8,2,128]{3,2,1,0:T(2,128)}, u32[]{:S(2)}, u32[]{:S(2)}) collective-permute-start(f32[6,8,2,128]{3,2,1,0:T(2,128)} %get-tuple-element.210), channel_id=1, source_target_pairs={{16,0},{17,1},{18,2},{19,3},{20,4},{21,5},{22,6},{23,7},{24,8},{25... | collective-permute-start | bytes 147464 | tf_op jit(solution)/shard_map/ppermute | solution.py:26
  131.3 1.9 collective-permute-start.4
  145.7 1.0 copy.444
  146.7 4.8 %collective-permute-start.8 = (f32[3,16,20,2]{2,1,3,0:T(8,128)}, f32[3,16,20,2]{2,1,3,0:T(8,128)S(1)}, u32[]{:S(2)}, u32[]{:S(2)}) collective-permute-start(f32[3,16,20,2]{2,1,3,0:T(8,128)} %copy.444), channel_id=1, source_target_pairs={{0,1},{1,2},{2,3},{3,4},{4,5},{5,6},{6,7},{7,8},{8,9},{9,10},{10,1... | collective-permute-start | bytes 23048 | tf_op jit(solution)/shard_map/ppermute | solution.py:25
  151.9 1.9 collective-permute-start.9
  156.2 6.2 %collective-permute-start.5 = (f32[6,2,8,128]{3,2,1,0:T(8,128)}, f32[6,2,8,128]{3,2,1,0:T(8,128)}, u32[]{:S(2)}, u32[]{:S(2)}) collective-permute-start(f32[6,2,8,128]{3,2,1,0:T(8,128)} %get-tuple-element.206), channel_id=1, source_target_pairs={{1,0},{2,1},{3,2},{5,4},{6,5},{7,6},{9,8},{10,9},{11,10},{13,12},{... | collective-permute-start | bytes 147464 | tf_op jit(solution)/shard_map/ppermute | solution.py:26
  162.8 1.2 copy.447
  167.2 1.5 slice_multiply_fusion.23
  168.7 1.1 slice_multiply_fusion.51
  171.3 2.2 %fusion.4 = f32[1,16,16,64]{3,2,1,0:T(8,128)S(1)} fusion(f32[1,16,16,64]{3,2,1,0:T(8,128)S(1)} %get-tuple-element.104, f32[16,130]{1,0:T(8,128)S(1)} %copy-done.253, s32[64]{0:T(128)S(1)} %copy-done.264, s32[64]{0:T(128)S(1)} %copy-done.265, f32[16,16,64]{2,1,0:T(8,128)S(1)} %get-tuple-element.107, f32[16,16,64]{2,1,0:T(8,128)} %copy-done.258, ...), kind=kOutput, calls=%fused_computation.5 | convolution fusion | flops 1653376 | bytes 570380 | tf_op jit(solution)/shard_map/dot_general | solution.py:222
  (844 shorter events, 110.3 us)
Async XLA Ops:
  2.3 142.2 %collective-permute-start.6 = (f32[3,16,2,64]{3,2,1,0:T(2,128)}, f32[3,16,2,64]{3,2,1,0:T(2,128)}, u32[]{:S(2)}, u32[]{:S(2)}) collective-permute-start(f32[3,16,2,64]{3,2,1,0:T(2,128)} %get-tuple-element.114), channel_id=1, source_target_pairs={{0,16},{1,17},{2,18},{3,19},{4,20},{5,21},{6,22},{7,23},{8,24},{9,... | collective-permute-start | bytes 73736 | tf_op jit(solution)/shard_map/ppermute | solution.py:25
  3.6 140.9 %collective-permute-start.7 = (f32[3,16,2,64]{3,2,1,0:T(2,128)}, f32[3,16,2,64]{3,2,1,0:T(2,128)}, u32[]{:S(2)}, u32[]{:S(2)}) collective-permute-start(f32[3,16,2,64]{3,2,1,0:T(2,128)} %get-tuple-element.115), channel_id=1, source_target_pairs={{16,0},{17,1},{18,2},{19,3},{20,4},{21,5},{22,6},{23,7},{24,8},{25... | collective-permute-start | bytes 73736 | tf_op jit(solution)/shard_map/ppermute | solution.py:26
  10.7 86.3 %collective-permute-start.10 = (f32[1,128]{1,0:T(1,128)}, f32[1,128]{1,0:T(1,128)}, u32[]{:S(2)}, u32[]{:S(2)}) collective-permute-start(f32[1,128]{1,0:T(1,128)} %get-tuple-element.134), channel_id=1, source_target_pairs={{0,16},{1,17},{2,18},{3,19},{4,20},{5,21},{6,22},{7,23},{8,24},{9,... | collective-permute-start | bytes 1544 | tf_op jit(solution)/shard_map/ppermute | solution.py:25
  12.0 7.3 %copy-start.1 = (f32[9,8,8,128]{3,2,1,0:T(8,128)S(1)}, f32[9,8,8,128]{3,2,1,0:T(8,128)}, u32[]{:S(2)}) copy-start(f32[9,8,8,128]{3,2,1,0:T(8,128)} %param.16) | copy-start | bytes 884740
  12.0 86.9 %collective-permute-start.11 = (f32[1,128]{1,0:T(1,128)}, f32[1,128]{1,0:T(1,128)}, u32[]{:S(2)}, u32[]{:S(2)}) collective-permute-start(f32[1,128]{1,0:T(1,128)} %get-tuple-element.135), channel_id=1, source_target_pairs={{16,0},{17,1},{18,2},{19,3},{20,4},{21,5},{22,6},{23,7},{24,8},{25... | collective-permute-start | bytes 1544 | tf_op jit(solution)/shard_map/ppermute | solution.py:26
  20.6 171.4 %collective-permute-start = (f32[6,8,2,128]{3,2,1,0:T(2,128)}, f32[6,8,2,128]{3,2,1,0:T(2,128)}, u32[]{:S(2)}, u32[]{:S(2)}) collective-permute-start(f32[6,8,2,128]{3,2,1,0:T(2,128)} %get-tuple-element.209), channel_id=1, source_target_pairs={{0,16},{1,17},{2,18},{3,19},{4,20},{5,21},{6,22},{7,23},{8,24},{9,... | collective-permute-start | bytes 147464 | tf_op jit(solution)/shard_map/ppermute | solution.py:25
  25.3 40.3 %copy-start.259 = (f32[16]{0:T(128)}, f32[16]{0:T(128)S(1)}, u32[]{:S(2)}) copy-start(f32[16]{0:T(128)S(1)} %get-tuple-element.500) | copy-start | bytes 196
  25.3 41.0 %copy-start.261 = (f32[16]{0:T(128)}, f32[16]{0:T(128)S(1)}, u32[]{:S(2)}) copy-start(f32[16]{0:T(128)S(1)} %get-tuple-element.501) | copy-start | bytes 196
  70.8 14.1 %copy-start.94 = (f32[8,8,1]{2,1,0:T(8,128)S(1)}, f32[8,8,1]{2,1,0:T(8,128)}, u32[]{:S(2)}) copy-start(f32[8,8,1]{2,1,0:T(8,128)} %get-tuple-element.420) | copy-start | bytes 772
  88.0 6.2 %copy-start.242 = (f32[8,1,128]{2,1,0:T(1,128)S(1)}, f32[8,1,128]{2,1,0:T(1,128)}, u32[]{:S(2)}) copy-start(f32[8,1,128]{2,1,0:T(1,128)} %get-tuple-element.360) | copy-start | bytes 12292
  88.0 6.2 %copy-start.243 = (f32[8,1,128]{2,1,0:T(1,128)S(1)}, f32[8,1,128]{2,1,0:T(1,128)}, u32[]{:S(2)}) copy-start(f32[8,1,128]{2,1,0:T(1,128)} %get-tuple-element.361) | copy-start | bytes 12292
  88.0 6.2 %copy-start.244 = (f32[8,1,128]{2,1,0:T(1,128)S(1)}, f32[8,1,128]{2,1,0:T(1,128)}, u32[]{:S(2)}) copy-start(f32[8,1,128]{2,1,0:T(1,128)} %get-tuple-element.364) | copy-start | bytes 12292
  88.0 6.2 %copy-start.245 = (f32[8,1,128]{2,1,0:T(1,128)S(1)}, f32[8,1,128]{2,1,0:T(1,128)}, u32[]{:S(2)}) copy-start(f32[8,1,128]{2,1,0:T(1,128)} %get-tuple-element.365) | copy-start | bytes 12292
  88.0 6.2 %copy-start.246 = (f32[8,1,128]{2,1,0:T(1,128)S(1)}, f32[8,1,128]{2,1,0:T(1,128)}, u32[]{:S(2)}) copy-start(f32[8,1,128]{2,1,0:T(1,128)} %get-tuple-element.367) | copy-start | bytes 12292
  88.0 6.2 %copy-start.247 = (f32[8,1,128]{2,1,0:T(1,128)S(1)}, f32[8,1,128]{2,1,0:T(1,128)}, u32[]{:S(2)}) copy-start(f32[8,1,128]{2,1,0:T(1,128)} %get-tuple-element.368) | copy-start | bytes 12292
  88.0 6.2 %copy-start.248 = (f32[8,1,128]{2,1,0:T(1,128)S(1)}, f32[8,1,128]{2,1,0:T(1,128)}, u32[]{:S(2)}) copy-start(f32[8,1,128]{2,1,0:T(1,128)} %get-tuple-element.369) | copy-start | bytes 12292
  88.1 5.4 %copy-start.225 = (f32[8,1,128]{2,1,0:T(1,128)S(1)}, f32[8,1,128]{2,1,0:T(1,128)}, u32[]{:S(2)}) copy-start(f32[8,1,128]{2,1,0:T(1,128)} %get-tuple-element.340) | copy-start | bytes 12292
  88.1 5.4 %copy-start.226 = (f32[8,1,128]{2,1,0:T(1,128)S(1)}, f32[8,1,128]{2,1,0:T(1,128)}, u32[]{:S(2)}) copy-start(f32[8,1,128]{2,1,0:T(1,128)} %get-tuple-element.399) | copy-start | bytes 12292
  88.9 5.9 %copy-start.74 = (f32[8,8,1]{2,1,0:T(8,128)S(1)}, f32[8,8,1]{2,1,0:T(8,128)}, u32[]{:S(2)}) copy-start(f32[8,8,1]{2,1,0:T(8,128)} %get-tuple-element.391) | copy-start | bytes 772
  97.0 28.6 %collective-permute-start.2 = (f32[6,8,8,2]{3,2,1,0:T(8,128)S(1)}, f32[6,8,8,2]{3,2,1,0:T(8,128)S(1)}, u32[]{:S(2)}, u32[]{:S(2)}) collective-permute-start(f32[6,8,8,2]{3,2,1,0:T(8,128)S(1)} %get-tuple-element.207), channel_id=1, source_target_pairs={{0,4},{4,8},{8,12},{1,5},{5,9},{9,13},{2,6},{6,10},{10,14},{3,7},{... | collective-permute-start | bytes 9224 | tf_op jit(solution)/shard_map/ppermute | solution.py:25
  99.7 5.0 %collective-permute-start.12 = (f32[10,1]{1,0:T(8,128)S(1)}, f32[10,1]{1,0:T(8,128)S(1)}, u32[]{:S(2)}, u32[]{:S(2)}) collective-permute-start(f32[10,1]{1,0:T(8,128)S(1)} %get-tuple-element.492), channel_id=1, source_target_pairs={{0,4},{4,8},{8,12},{1,5},{5,9},{9,13},{2,6},{6,10},{10,14},{3,7},{... | collective-permute-start | bytes 128 | tf_op jit(solution)/shard_map/ppermute | solution.py:25
  104.6 3.3 %collective-permute-start.13 = (f32[10,1]{1,0:T(8,128)S(1)}, f32[10,1]{1,0:T(8,128)S(1)}, u32[]{:S(2)}, u32[]{:S(2)}) collective-permute-start(f32[10,1]{1,0:T(8,128)S(1)} %get-tuple-element.493), channel_id=1, source_target_pairs={{4,0},{8,4},{12,8},{5,1},{9,5},{13,9},{6,2},{10,6},{14,10},{7,3},{... | collective-permute-start | bytes 128 | tf_op jit(solution)/shard_map/ppermute | solution.py:26
  107.9 23.4 %collective-permute-start.3 = (f32[6,8,8,2]{3,2,1,0:T(8,128)S(1)}, f32[6,8,8,2]{3,2,1,0:T(8,128)S(1)}, u32[]{:S(2)}, u32[]{:S(2)}) collective-permute-start(f32[6,8,8,2]{3,2,1,0:T(8,128)S(1)} %get-tuple-element.208), channel_id=1, source_target_pairs={{4,0},{8,4},{12,8},{5,1},{9,5},{13,9},{6,2},{10,6},{14,10},{7,3},{... | collective-permute-start | bytes 9224 | tf_op jit(solution)/shard_map/ppermute | solution.py:26
  124.7 8.5 %copy-start.34 = (f32[1,8,8,128]{3,2,1,0:T(8,128)S(1)}, f32[1,8,8,128]{3,2,1,0:T(8,128)}, u32[]{:S(2)}) copy-start(f32[1,8,8,128]{3,2,1,0:T(8,128)} %copy-done.33) | copy-start | bytes 98308
  124.7 8.5 %copy-start.36 = (f32[1,8,8,128]{3,2,1,0:T(8,128)S(1)}, f32[1,8,8,128]{3,2,1,0:T(8,128)}, u32[]{:S(2)}) copy-start(f32[1,8,8,128]{3,2,1,0:T(8,128)} %copy-done.35) | copy-start | bytes 98308
  125.5 66.4 %collective-permute-start.1 = (f32[6,8,2,128]{3,2,1,0:T(2,128)}, f32[6,8,2,128]{3,2,1,0:T(2,128)}, u32[]{:S(2)}, u32[]{:S(2)}) collective-permute-start(f32[6,8,2,128]{3,2,1,0:T(2,128)} %get-tuple-element.210), channel_id=1, source_target_pairs={{16,0},{17,1},{18,2},{19,3},{20,4},{21,5},{22,6},{23,7},{24,8},{25... | collective-permute-start | bytes 147464 | tf_op jit(solution)/shard_map/ppermute | solution.py:26
  131.3 59.7 %collective-permute-start.4 = (f32[6,2,8,128]{3,2,1,0:T(8,128)}, f32[6,2,8,128]{3,2,1,0:T(8,128)}, u32[]{:S(2)}, u32[]{:S(2)}) collective-permute-start(f32[6,2,8,128]{3,2,1,0:T(8,128)} %get-tuple-element.205), channel_id=1, source_target_pairs={{0,1},{1,2},{2,3},{4,5},{5,6},{6,7},{8,9},{9,10},{10,11},{12,13},{... | collective-permute-start | bytes 147464 | tf_op jit(solution)/shard_map/ppermute | solution.py:25
  146.7 9.4 %collective-permute-start.8 = (f32[3,16,20,2]{2,1,3,0:T(8,128)}, f32[3,16,20,2]{2,1,3,0:T(8,128)S(1)}, u32[]{:S(2)}, u32[]{:S(2)}) collective-permute-start(f32[3,16,20,2]{2,1,3,0:T(8,128)} %copy.444), channel_id=1, source_target_pairs={{0,1},{1,2},{2,3},{3,4},{4,5},{5,6},{6,7},{7,8},{8,9},{9,10},{10,1... | collective-permute-start | bytes 23048 | tf_op jit(solution)/shard_map/ppermute | solution.py:25
  151.9 10.8 %collective-permute-start.9 = (f32[3,16,20,2]{2,1,3,0:T(8,128)S(1)}, f32[3,16,20,2]{2,1,3,0:T(8,128)}, u32[]{:S(2)}, u32[]{:S(2)}) collective-permute-start(f32[3,16,20,2]{2,1,3,0:T(8,128)S(1)} %copy.445), channel_id=1, source_target_pairs={{1,0},{2,1},{3,2},{4,3},{5,4},{6,5},{7,6},{8,7},{9,8},{10,9},{11,1... | collective-permute-start | bytes 23048 | tf_op jit(solution)/shard_map/ppermute | solution.py:26
  156.1 9.4 %copy-start.52 = (f32[16,4,64]{2,1,0:T(4,128)}, f32[16,4,64]{2,1,0:T(4,128)S(1)}, u32[]{:S(2)}) copy-start(f32[16,4,64]{2,1,0:T(4,128)S(1)} %get-tuple-element.255) | copy-start | bytes 49156
  156.1 9.4 %copy-start.54 = (f32[16,4,64]{2,1,0:T(4,128)}, f32[16,4,64]{2,1,0:T(4,128)S(1)}, u32[]{:S(2)}) copy-start(f32[16,4,64]{2,1,0:T(4,128)S(1)} %get-tuple-element.256) | copy-start | bytes 49156
  156.2 34.8 %collective-permute-start.5 = (f32[6,2,8,128]{3,2,1,0:T(8,128)}, f32[6,2,8,128]{3,2,1,0:T(8,128)}, u32[]{:S(2)}, u32[]{:S(2)}) collective-permute-start(f32[6,2,8,128]{3,2,1,0:T(8,128)} %get-tuple-element.206), channel_id=1, source_target_pairs={{1,0},{2,1},{3,2},{5,4},{6,5},{7,6},{9,8},{10,9},{11,10},{13,12},{... | collective-permute-start | bytes 147464 | tf_op jit(solution)/shard_map/ppermute | solution.py:26
  (250 other events, 306.9 us)
